TPU v7x, 32 devices: a whole 2x2x4 slice. The times are simulated.
32 devices in a mesh: shard: 4 (over y, x), rep: 8 (over z, core).
Axes of the slice: x: 2, y: 2, z: 4, core: 2. Of those that a mesh axis runs over, the one named last changes fastest.
Arguments:
- latents: bfloat16 [32, 256, 384], P(('shard', 'rep')), may hold values from -6 to 6
- condition: bfloat16 [32, 384], P(('shard', 'rep')), may hold values from -4 to 4
- cotangent: bfloat16 [32, 256, 384], P(('shard', 'rep')), may hold values from -6 to 6
- w_qkv: bfloat16 [2, 384, 1152], P(None, 'shard'), may hold values from -0.15625 to 0.15625
- b_qv: bfloat16 [2, 768], P(None, 'shard'), may hold values from -3 to 3
- w_proj: bfloat16 [2, 384, 384], P(None, 'shard'), may hold values from -1.75 to 1.75
- b_proj: bfloat16 [2, 384], P(None, 'shard'), may hold values from -3 to 3
- w_fc1: bfloat16 [2, 384, 1536], P(None, 'shard'), may hold values from -0.3125 to 0.3125
- b_fc1: bfloat16 [2, 1536], P(None, 'shard'), may hold values from -3 to 3
- w_fc2: bfloat16 [2, 1536, 384], P(None, 'shard'), may hold values from -0.15625 to 0.15625
- b_fc2: bfloat16 [2, 384], P(None, 'shard'), may hold values from -3 to 3
- w_ada: bfloat16 [2, 384, 2304], P(None, 'shard'), may hold values from -4 to 4
- b_ada: bfloat16 [2, 2304], P(None, 'shard'), may hold values from -3 to 3
Outputs:
- x_out: bfloat16 [32, 256, 384], P(('shard', 'rep'))
- x_grad: float32 [32, 256, 384], P(('shard', 'rep'))
- cond_grad: float32 [32, 384], P(('shard', 'rep'))
- grad_qkv: float32 [2, 384, 1152], P(None, 'shard')
- grad_qv_bias: float32 [2, 768], P(None, 'shard')
- grad_proj: float32 [2, 384, 384], P(None, 'shard')
- grad_proj_bias: float32 [2, 384], P(None, 'shard')
- grad_fc1: float32 [2, 384, 1536], P(None, 'shard')
- grad_fc1_bias: float32 [2, 1536], P(None, 'shard')
- grad_fc2: float32 [2, 1536, 384], P(None, 'shard')
- grad_fc2_bias: float32 [2, 384], P(None, 'shard')
- grad_ada: float32 [2, 384, 2304], P(None, 'shard')
- grad_ada_bias: float32 [2, 2304], P(None, 'shard')
All inputs are finite; a program needn't handle non-finite values.
Results may differ from a plain program's by a relative error of at most 0.017.
Values may be sent and summed in bfloat16 or wider, within the bound.
No kernel may reach another device: no remote copies, remote signals or barrier semaphores. Data moves between devices by JAX's collectives and lax.ppermute only.
A program may use at most 128 MiB of HBM per device.

v0:
```python
import jax
import jax.numpy as jnp
from jax import lax
from jax.sharding import PartitionSpec as P

HEADS = 6


def layer_norm(residual_state):
    center = residual_state - jnp.mean(residual_state, axis=-1, keepdims=True)
    inverse = lax.rsqrt(jnp.mean(center * center, axis=-1, keepdims=True) + 1e-06)
    return (center * inverse, inverse)


def norm_back(grad_norm, normed, inverse):
    centered = grad_norm - jnp.mean(grad_norm, axis=-1, keepdims=True)
    return inverse * (centered - normed * jnp.mean(grad_norm * normed, axis=-1, keepdims=True))


def project(left, right):
    return jnp.einsum("lsd,de->lse", left, right, preferred_element_type=jnp.float32)


def project_back(left, right):
    return jnp.einsum("lse,de->lsd", left, right, preferred_element_type=jnp.float32)


def weight_grad(left, right):
    return jnp.einsum("lsd,lse->de", left, right, preferred_element_type=jnp.float32)


def column_sums(grad_low):
    return jnp.sum(grad_low.astype(jnp.float32), axis=(0, 1))


def split_heads(tensor):
    return tensor.reshape(tensor.shape[0], tensor.shape[1], HEADS, tensor.shape[2] // HEADS)


def forward_layer(gathered, residual_state, condition_activation):
    w_qkv, b_qv, w_proj, b_proj, w_fc1, b_fc1, w_fc2, b_fc2, w_ada, b_ada = gathered
    width = residual_state.shape[2]
    modulate = jnp.dot(
        condition_activation, w_ada, preferred_element_type=jnp.float32
    ) + b_ada.astype(jnp.float32)
    pieces = [part_mod[:, None, :] for part_mod in jnp.split(modulate, 6, axis=-1)]
    shift_one, scale_one, gate_one, shift_two, scale_two, gate_two = pieces
    normed_one, inverse_one = layer_norm(residual_state)
    h_one = (normed_one * (1.0 + scale_one) + shift_one).astype(jnp.bfloat16)
    mixed = project(h_one, w_qkv)
    bias_wide = b_qv.astype(jnp.float32)
    queries = split_heads((mixed[..., :width] + bias_wide[:width]).astype(jnp.bfloat16))
    key_rows = split_heads(mixed[..., width : 2 * width].astype(jnp.bfloat16))
    value_rows = split_heads((mixed[..., 2 * width :] + bias_wide[width:]).astype(jnp.bfloat16))
    scale_dot = (width // HEADS) ** (-0.5)
    scores = (
        jnp.einsum("lqhd,lkhd->lhqk", queries, key_rows, preferred_element_type=jnp.float32)
        * scale_dot
    )
    top_score = jnp.max(scores, axis=-1, keepdims=True)
    log_total = top_score + jnp.log(jnp.sum(jnp.exp(scores - top_score), axis=-1, keepdims=True))
    probs_low = jnp.exp(scores - log_total).astype(jnp.bfloat16)
    attended = jnp.einsum(
        "lhqk,lkhd->lqhd", probs_low, value_rows, preferred_element_type=jnp.float32
    )
    attended = attended.reshape(residual_state.shape).astype(jnp.bfloat16)
    branch = project(attended, w_proj) + b_proj.astype(jnp.float32)
    middle = residual_state + gate_one * branch
    normed_two, inverse_two = layer_norm(middle)
    h_two = (normed_two * (1.0 + scale_two) + shift_two).astype(jnp.bfloat16)
    pre_act = project(h_two, w_fc1) + b_fc1.astype(jnp.float32)
    act_low = jax.nn.gelu(pre_act, approximate=True).astype(jnp.bfloat16)
    mlp_out = project(act_low, w_fc2) + b_fc2.astype(jnp.float32)
    stream_next = middle + gate_two * mlp_out
    stored = (
        pieces,
        normed_one,
        inverse_one,
        h_one,
        queries,
        key_rows,
        value_rows,
        log_total,
        attended,
        branch,
        normed_two,
        inverse_two,
        h_two,
        pre_act,
        act_low,
        mlp_out,
    )
    return (stream_next, stored)


def backward_layer(gathered, stored, grad_out, condition_activation):
    w_qkv, b_qv, w_proj, b_proj, w_fc1, b_fc1, w_fc2, b_fc2, w_ada, b_ada = gathered
    (
        pieces,
        normed_one,
        inverse_one,
        h_one,
        queries,
        key_rows,
        value_rows,
        log_total,
        attended,
        branch,
        normed_two,
        inverse_two,
        h_two,
        pre_act,
        act_low,
        mlp_out,
    ) = stored
    shift_one, scale_one, gate_one, shift_two, scale_two, gate_two = pieces
    width = grad_out.shape[2]
    scale_dot = (width // HEADS) ** (-0.5)
    d_gate_two = jnp.sum(grad_out * mlp_out, axis=1)
    d_mlp = (grad_out * gate_two).astype(jnp.bfloat16)
    g_fc2 = weight_grad(act_low, d_mlp)
    gb_fc2 = column_sums(d_mlp)
    d_act = project_back(d_mlp, w_fc2)
    gelu_pull = jax.vjp(lambda pre_in: jax.nn.gelu(pre_in, approximate=True), pre_act)[1]
    d_pre = gelu_pull(d_act)[0].astype(jnp.bfloat16)
    g_fc1 = weight_grad(h_two, d_pre)
    gb_fc1 = column_sums(d_pre)
    d_h_two = project_back(d_pre, w_fc1)
    d_shift_two = jnp.sum(d_h_two, axis=1)
    d_scale_two = jnp.sum(d_h_two * normed_two, axis=1)
    d_middle = grad_out + norm_back(d_h_two * (1.0 + scale_two), normed_two, inverse_two)
    d_gate_one = jnp.sum(d_middle * branch, axis=1)
    d_branch = (d_middle * gate_one).astype(jnp.bfloat16)
    g_proj = weight_grad(attended, d_branch)
    gb_proj = column_sums(d_branch)
    d_attended = split_heads(project_back(d_branch, w_proj).astype(jnp.bfloat16))
    scores = (
        jnp.einsum("lqhd,lkhd->lhqk", queries, key_rows, preferred_element_type=jnp.float32)
        * scale_dot
    )
    probs = jnp.exp(scores - log_total)
    probs_low = probs.astype(jnp.bfloat16)
    d_values = jnp.einsum(
        "lhqk,lqhd->lkhd", probs_low, d_attended, preferred_element_type=jnp.float32
    )
    d_probs = jnp.einsum(
        "lqhd,lkhd->lhqk", d_attended, value_rows, preferred_element_type=jnp.float32
    )
    d_scores = (probs * (d_probs - jnp.sum(probs * d_probs, axis=-1, keepdims=True))).astype(
        jnp.bfloat16
    )
    d_queries = (
        jnp.einsum("lhqk,lkhd->lqhd", d_scores, key_rows, preferred_element_type=jnp.float32)
        * scale_dot
    )
    d_keys = (
        jnp.einsum("lhqk,lqhd->lkhd", d_scores, queries, preferred_element_type=jnp.float32)
        * scale_dot
    )
    flat_shape = grad_out.shape
    d_qkv = jnp.concatenate(
        [d_queries.reshape(flat_shape), d_keys.reshape(flat_shape), d_values.reshape(flat_shape)],
        axis=-1,
    ).astype(jnp.bfloat16)
    g_qkv = weight_grad(h_one, d_qkv)
    qkv_sums = column_sums(d_qkv)
    gb_qv = jnp.concatenate([qkv_sums[:width], qkv_sums[2 * width :]])
    d_h_one = project_back(d_qkv, w_qkv)
    d_shift_one = jnp.sum(d_h_one, axis=1)
    d_scale_one = jnp.sum(d_h_one * normed_one, axis=1)
    d_stream = d_middle + norm_back(d_h_one * (1.0 + scale_one), normed_one, inverse_one)
    d_mod = jnp.concatenate(
        [d_shift_one, d_scale_one, d_gate_one, d_shift_two, d_scale_two, d_gate_two], axis=-1
    ).astype(jnp.bfloat16)
    g_ada = jnp.einsum("ld,le->de", condition_activation, d_mod, preferred_element_type=jnp.float32)
    gb_ada = jnp.sum(d_mod.astype(jnp.float32), axis=0)
    d_cond = jnp.einsum("le,de->ld", d_mod, w_ada, preferred_element_type=jnp.float32)
    grads = (g_qkv, gb_qv, g_proj, gb_proj, g_fc1, gb_fc1, g_fc2, gb_fc2, g_ada, gb_ada)
    return (d_stream, d_cond, grads)


def shards(
    latents,
    condition,
    cotangent,
    w_qkv,
    b_qv,
    w_proj,
    b_proj,
    w_fc1,
    b_fc1,
    w_fc2,
    b_fc2,
    w_ada,
    b_ada,
):
    layers = w_qkv.shape[0]
    total_latents = latents.shape[0] * lax.axis_size("shard") * lax.axis_size("rep")
    cond_in = condition.astype(jnp.float32)
    condition_activation = jax.nn.silu(cond_in).astype(jnp.bfloat16)
    residual_state = latents.astype(jnp.float32)
    gathered_all = []
    stored_all = []
    for layer_number in range(layers):
        gathered = (
            lax.all_gather(w_qkv[layer_number], "shard", axis=0, tiled=True),
            lax.all_gather(b_qv[layer_number], "shard", axis=0, tiled=True),
            lax.all_gather(w_proj[layer_number], "shard", axis=0, tiled=True),
            lax.all_gather(b_proj[layer_number], "shard", axis=0, tiled=True),
            lax.all_gather(w_fc1[layer_number], "shard", axis=0, tiled=True),
            lax.all_gather(b_fc1[layer_number], "shard", axis=0, tiled=True),
            lax.all_gather(w_fc2[layer_number], "shard", axis=0, tiled=True),
            lax.all_gather(b_fc2[layer_number], "shard", axis=0, tiled=True),
            lax.all_gather(w_ada[layer_number], "shard", axis=0, tiled=True),
            lax.all_gather(b_ada[layer_number], "shard", axis=0, tiled=True),
        )
        residual_state, stored = forward_layer(gathered, residual_state, condition_activation)
        gathered_all.append(gathered)
        stored_all.append(stored)
    x_out = residual_state.astype(jnp.bfloat16)
    grad_stream = cotangent.astype(jnp.float32)
    grad_cond = jnp.zeros(cond_in.shape, jnp.float32)
    collected = []
    for layer_number in reversed(range(layers)):
        gathered = (
            lax.all_gather(w_qkv[layer_number], "shard", axis=0, tiled=True),
            lax.all_gather(b_qv[layer_number], "shard", axis=0, tiled=True),
            lax.all_gather(w_proj[layer_number], "shard", axis=0, tiled=True),
            lax.all_gather(b_proj[layer_number], "shard", axis=0, tiled=True),
            lax.all_gather(w_fc1[layer_number], "shard", axis=0, tiled=True),
            lax.all_gather(b_fc1[layer_number], "shard", axis=0, tiled=True),
            lax.all_gather(w_fc2[layer_number], "shard", axis=0, tiled=True),
            lax.all_gather(b_fc2[layer_number], "shard", axis=0, tiled=True),
            lax.all_gather(w_ada[layer_number], "shard", axis=0, tiled=True),
            lax.all_gather(b_ada[layer_number], "shard", axis=0, tiled=True),
        )
        grad_stream, d_cond, grads = backward_layer(
            gathered, stored_all[layer_number], grad_stream, condition_activation
        )
        grad_cond = grad_cond + d_cond
        owner_rows = (
            lax.psum_scatter(
                grads[0].astype(jnp.bfloat16), "shard", scatter_dimension=0, tiled=True
            ).astype(jnp.float32),
            lax.psum_scatter(
                grads[1].astype(jnp.bfloat16), "shard", scatter_dimension=0, tiled=True
            ).astype(jnp.float32),
            lax.psum_scatter(
                grads[2].astype(jnp.bfloat16), "shard", scatter_dimension=0, tiled=True
            ).astype(jnp.float32),
            lax.psum_scatter(
                grads[3].astype(jnp.bfloat16), "shard", scatter_dimension=0, tiled=True
            ).astype(jnp.float32),
            lax.psum_scatter(
                grads[4].astype(jnp.bfloat16), "shard", scatter_dimension=0, tiled=True
            ).astype(jnp.float32),
            lax.psum_scatter(
                grads[5].astype(jnp.bfloat16), "shard", scatter_dimension=0, tiled=True
            ).astype(jnp.float32),
            lax.psum_scatter(
                grads[6].astype(jnp.bfloat16), "shard", scatter_dimension=0, tiled=True
            ).astype(jnp.float32),
            lax.psum_scatter(
                grads[7].astype(jnp.bfloat16), "shard", scatter_dimension=0, tiled=True
            ).astype(jnp.float32),
            lax.psum_scatter(
                grads[8].astype(jnp.bfloat16), "shard", scatter_dimension=0, tiled=True
            ).astype(jnp.float32),
            lax.psum_scatter(
                grads[9].astype(jnp.bfloat16), "shard", scatter_dimension=0, tiled=True
            ).astype(jnp.float32),
        )
        owner_rows = (
            lax.psum(owner_rows[0].astype(jnp.bfloat16), "rep").astype(jnp.float32),
            lax.psum(owner_rows[1].astype(jnp.bfloat16), "rep").astype(jnp.float32),
            lax.psum(owner_rows[2].astype(jnp.bfloat16), "rep").astype(jnp.float32),
            lax.psum(owner_rows[3].astype(jnp.bfloat16), "rep").astype(jnp.float32),
            lax.psum(owner_rows[4].astype(jnp.bfloat16), "rep").astype(jnp.float32),
            lax.psum(owner_rows[5].astype(jnp.bfloat16), "rep").astype(jnp.float32),
            lax.psum(owner_rows[6].astype(jnp.bfloat16), "rep").astype(jnp.float32),
            lax.psum(owner_rows[7].astype(jnp.bfloat16), "rep").astype(jnp.float32),
            lax.psum(owner_rows[8].astype(jnp.bfloat16), "rep").astype(jnp.float32),
            lax.psum(owner_rows[9].astype(jnp.bfloat16), "rep").astype(jnp.float32),
        )
        collected.insert(0, owner_rows)
    stacked = [
        jnp.stack([layer_rows[slot_no] for layer_rows in collected]) for slot_no in range(10)
    ]
    silu_pull = jax.vjp(jax.nn.silu, cond_in)[1]
    cond_grad = silu_pull(grad_cond)[0]
    inverse_count = 1.0 / total_latents
    return (
        x_out,
        grad_stream,
        cond_grad,
        stacked[0] * inverse_count,
        stacked[1] * inverse_count,
        stacked[2] * inverse_count,
        stacked[3] * inverse_count,
        stacked[4] * inverse_count,
        stacked[5] * inverse_count,
        stacked[6] * inverse_count,
        stacked[7] * inverse_count,
        stacked[8] * inverse_count,
        stacked[9] * inverse_count,
    )


def solution(mesh):
    return jax.shard_map(
        shards,
        mesh=mesh,
        in_specs=(
            P(("shard", "rep"), None, None),
            P(("shard", "rep"), None),
            P(("shard", "rep"), None, None),
            P(None, "shard", None),
            P(None, "shard"),
            P(None, "shard", None),
            P(None, "shard"),
            P(None, "shard", None),
            P(None, "shard"),
            P(None, "shard", None),
            P(None, "shard"),
            P(None, "shard", None),
            P(None, "shard"),
        ),
        out_specs=(
            P(("shard", "rep"), None, None),
            P(("shard", "rep"), None, None),
            P(("shard", "rep"), None),
            P(None, "shard", None),
            P(None, "shard"),
            P(None, "shard", None),
            P(None, "shard"),
            P(None, "shard", None),
            P(None, "shard"),
            P(None, "shard", None),
            P(None, "shard"),
            P(None, "shard", None),
            P(None, "shard"),
        ),
        check_vma=False,
    )
```

profile of v0, /device:TPU:0, one launch (start us, length us, event | category | flops | bytes accessed | tf_op | source)
XLA Modules:
  0.0 625.9 jit_solution(534134971308301505)
XLA Ops:
  17.0 9.5 %all-gather.17 = bf16[1,1536]{1,0:T(2,128)(2,1)S(1)} all-gather(bf16[1,384]{1,0:T(2,128)(2,1)S(1)} %get-tuple-element.131), channel_id=19, replica_groups=mesh['shard'=4,'rep'=8] {'shard'}, dimensions={1}, use_global_device_ids=true | all-gather | bytes 3840 | tf_op jit(solution)/shard_map/all_gather | solution.py:211
  27.2 8.0 %all-gather.7 = bf16[1,1536]{1,0:T(2,128)(2,1)S(1)} all-gather(bf16[1,384]{1,0:T(2,128)(2,1)S(1)} %get-tuple-element.132), channel_id=9, replica_groups=mesh['shard'=4,'rep'=8] {'shard'}, dimensions={1}, use_global_device_ids=true | all-gather | bytes 3840 | tf_op jit(solution)/shard_map/all_gather | solution.py:211
  37.5 15.8 %all-reduce.21 = (bf16[2304]{0:T(1024)(128)(2,1)S(1)}, bf16[768]{0:T(1024)(128)(2,1)S(1)}, bf16[384]{0:T(512)(128)(2,1)S(1)}, bf16[384]{0:T(512)(128)(2,1)S(1)},...) all-reduce(bf16[2304]{0:T(1024)(128)(2,1)S(1)} %dynamic-update-slic, ...), channel_id=3, replica_groups=mesh['shard'=4,'rep'=8] {'shard'}, use_global_device_ids=true, to_apply=%add | all-reduce | flops 7680 | bytes 30720
  56.3 10.3 %all-gather.14 = bf16[1,384,384]{2,1,0:T(8,128)(2,1)} all-gather(bf16[1,96,384]{2,1,0:T(8,128)(2,1)S(1)} %get-tuple-element.123), channel_id=16, replica_groups=mesh['shard'=4,'rep'=8] {'shard'}, dimensions={1}, use_global_device_ids=true | all-gather | bytes 368640 | tf_op jit(solution)/shard_map/all_gather | solution.py:208
  66.6 11.1 %all-gather.4 = bf16[1,384,384]{2,1,0:T(8,128)(2,1)S(1)} all-gather(bf16[1,96,384]{2,1,0:T(8,128)(2,1)S(1)} %get-tuple-element.124), channel_id=6, replica_groups=mesh['shard'=4,'rep'=8] {'shard'}, dimensions={1}, use_global_device_ids=true | all-gather | bytes 368640 | tf_op jit(solution)/shard_map/all_gather | solution.py:208
  77.7 14.5 %all-gather.12 = bf16[1,384,1152]{2,1,0:T(8,128)(2,1)S(1)} all-gather(bf16[1,96,1152]{2,1,0:T(8,128)(2,1)S(1)} %get-tuple-element.114), channel_id=14, replica_groups=mesh['shard'=4,'rep'=8] {'shard'}, dimensions={1}, use_global_device_ids=true | all-gather | bytes 1105920 | tf_op jit(solution)/shard_map/all_gather | solution.py:206
  92.2 14.5 %all-gather.2 = bf16[1,384,1152]{2,1,0:T(8,128)(2,1)S(1)} all-gather(bf16[1,96,1152]{2,1,0:T(8,128)(2,1)S(1)} %get-tuple-element.115), channel_id=4, replica_groups=mesh['shard'=4,'rep'=8] {'shard'}, dimensions={1}, use_global_device_ids=true | all-gather | bytes 1105920 | tf_op jit(solution)/shard_map/all_gather | solution.py:206
  115.7 4.5 all-gather.29.cloned.1.call-done
  120.2 3.0 convolution_add_fusion.1
  123.2 26.4 %all-gather.31.cloned.1.call-done = bf16[1,1536,384]{2,1,0:T(8,128)(2,1)} async-done(((bf16[1,384,384]{2,1,0:T(8,128)(2,1)}), bf16[1,1536,384]{2,1,0:T(8,128)(2,1)}) %all-gather.31.cloned.1.call-update) | async-done | bytes 1179664 | tf_op jit(solution)/shard_map/all_gather | solution.py:212
  149.6 3.2 fusion.152
  161.5 17.6 %all-gather.35.cloned.1.call-done = bf16[1,384,1536]{2,1,0:T(8,128)(2,1)} async-done(((bf16[1,96,1536]{2,1,0:T(8,128)(2,1)}), bf16[1,384,1536]{2,1,0:T(8,128)(2,1)}) %all-gather.35.cloned.1.call-update) | async-done | bytes 1179664 | tf_op jit(solution)/shard_map/all_gather | solution.py:210
  179.0 3.2 convolution_add_fusion
  182.2 26.9 %all-gather.37.cloned.1.call-done = bf16[1,1536,384]{2,1,0:T(8,128)(2,1)} async-done(((bf16[1,384,384]{2,1,0:T(8,128)(2,1)}), bf16[1,1536,384]{2,1,0:T(8,128)(2,1)}) %all-gather.37.cloned.1.call-update) | async-done | bytes 1179664 | tf_op jit(solution)/shard_map/all_gather | solution.py:212
  209.1 4.0 fusion.165
  226.8 2.5 fusion.87
  238.2 2.7 convolution_convert_fusion
  246.9 3.3 convolution_convert_fusion.2
  253.1 3.2 convolution_convert_fusion.3
  256.5 2.8 convolution_convert_fusion.5
  264.4 2.8 multiply_convert_fusion.1
  278.0 30.3 %reduce-scatter.13.cloned.1.call-done = bf16[96,1152]{1,0:T(8,128)(2,1)} async-done(((bf16[384,1152]{1,0:T(8,128)(2,1)}), bf16[96,1152]{1,0:T(8,128)(2,1)}) %reduce-scatter.13.cloned.1.call-update) | async-done | bytes 221200 | tf_op jit(solution)/shard_map/reduce_scatter | solution.py:242
  308.3 29.5 %reduce-scatter.11.cloned.1.call-done = bf16[96,1152]{1,0:T(8,128)(2,1)} async-done(((bf16[384,1152]{1,0:T(8,128)(2,1)}), bf16[96,1152]{1,0:T(8,128)(2,1)}) %reduce-scatter.11.cloned.1.call-update) | async-done | bytes 221200 | tf_op jit(solution)/shard_map/reduce_scatter | solution.py:242
  337.8 31.5 %reduce-scatter.25.cloned.1.call-done = bf16[384,384]{1,0:T(8,128)(2,1)} async-done(((bf16[1536,384]{1,0:T(8,128)(2,1)}), bf16[384,384]{1,0:T(8,128)(2,1)}) %reduce-scatter.25.cloned.1.call-update) | async-done | bytes 294928 | tf_op jit(solution)/shard_map/reduce_scatter | solution.py:260
  369.3 31.9 %reduce-scatter.21.cloned.1.call-done = bf16[96,1536]{1,0:T(8,128)(2,1)} async-done(((bf16[384,1536]{1,0:T(8,128)(2,1)}), bf16[96,1536]{1,0:T(8,128)(2,1)}) %reduce-scatter.21.cloned.1.call-update) | async-done | bytes 294928 | tf_op jit(solution)/shard_map/reduce_scatter | solution.py:254
  401.2 31.5 %reduce-scatter.23.cloned.1.call-done = bf16[384,384]{1,0:T(8,128)(2,1)} async-done(((bf16[1536,384]{1,0:T(8,128)(2,1)}), bf16[384,384]{1,0:T(8,128)(2,1)}) %reduce-scatter.23.cloned.1.call-update) | async-done | bytes 294928 | tf_op jit(solution)/shard_map/reduce_scatter | solution.py:260
  432.7 31.9 %reduce-scatter.19.cloned.1.call-done = bf16[96,1536]{1,0:T(8,128)(2,1)} async-done(((bf16[384,1536]{1,0:T(8,128)(2,1)}), bf16[96,1536]{1,0:T(8,128)(2,1)}) %reduce-scatter.19.cloned.1.call-update) | async-done | bytes 294928 | tf_op jit(solution)/shard_map/reduce_scatter | solution.py:254
  464.6 36.0 %reduce-scatter.27.cloned.1.call-done = bf16[96,2304]{1,0:T(8,128)(2,1)} async-done(((bf16[384,2304]{1,0:T(8,128)(2,1)}), bf16[96,2304]{1,0:T(8,128)(2,1)}) %reduce-scatter.27.cloned.1.call-update) | async-done | bytes 442384 | tf_op jit(solution)/shard_map/reduce_scatter | solution.py:266
  500.6 35.4 %reduce-scatter.29.cloned.1.call-done = bf16[96,2304]{1,0:T(8,128)(2,1)} async-done(((bf16[384,2304]{1,0:T(8,128)(2,1)}), bf16[96,2304]{1,0:T(8,128)(2,1)}) %reduce-scatter.29.cloned.1.call-update) | async-done | bytes 442384 | tf_op jit(solution)/shard_map/reduce_scatter | solution.py:266
  536.1 15.3 %all-reduce.20 = (bf16[768]{0:T(1024)(128)(2,1)S(1)}, bf16[768]{0:T(1024)(128)(2,1)S(1)}, bf16[384]{0:T(512)(128)(2,1)S(1)}, bf16[384]{0:T(512)(128)(2,1)S(1)}, ...) all-reduce(bf16[768]{0:T(1024)(128)(2,1)S(1)} %copy-done.118, ...), channel_id=25, replica_groups=mesh['shard'=4,'rep'=8] {'shard'}, use_global_device_ids=true, to_apply=%region_42.43.clone | all-reduce | flops 10752 | bytes 43008
  552.3 27.0 %all-reduce.18 = (bf16[1,192]{1,0:T(2,128)(2,1)S(1)}, bf16[1,192]{1,0:T(2,128)(2,1)S(1)}, bf16[1,96]{1,0:T(2,128)(2,1)S(1)}, bf16[1,96]{1,0:T(2,128)(2,1)S(1)}, ...) all-reduce(bf16[1,192]{1,0:T(2,128)(2,1)S(1)} %stack.145, ...), channel_id=1, replica_groups=mesh['shard'=4,'rep'=8] {'rep'}, use_global_device_ids=true, to_apply=%region_43.44 | all-reduce | flops 2688 | bytes 10752 | tf_op jit(solution)/shard_map/psum | solution.py:275
  582.8 29.2 %all-reduce.24.cloned.1.call-done = (bf16[1,96,1152]{2,1,0:T(8,128)(2,1)}, bf16[1,96,1152]{2,1,0:T(8,128)(2,1)}, bf16[1,96,384]{2,1,0:T(8,128)(2,1)}, bf16[1,96,...) async-done(((bf16[1,96,1152]{2,1,0:T(8,128)(2,1)}, ...) | async-done | bytes 2654224 | tf_op jit(solution)/shard_map/psum | solution.py:274
  (503 shorter events, 86.7 us)
Async XLA Ops:
  7.2 99.5 %all-gather.27.cloned.1.call-start = ((), (), s32[]{:S(2)}) async-start(), calls=%async_computation.20 | async-start | bytes 2211840 | tf_op jit(solution)/shard_map/all_gather | solution.py:214
  9.4 99.4 %all-gather.33.cloned.1.call-start = ((), (), s32[]{:S(2)}) async-start(), calls=%async_computation.23 | async-start | bytes 2211840 | tf_op jit(solution)/shard_map/all_gather | solution.py:214
  10.2 110.0 %all-gather.29.cloned.1.call-start = ((), (), s32[]{:S(2)}) async-start(), calls=%async_computation.21 | async-start | bytes 1474560 | tf_op jit(solution)/shard_map/all_gather | solution.py:210
  11.2 138.4 %all-gather.31.cloned.1.call-start = ((), (), s32[]{:S(2)}) async-start(), calls=%async_computation.22 | async-start | bytes 1474560 | tf_op jit(solution)/shard_map/all_gather | solution.py:212
  12.1 65.5 %copy-start.53 = (bf16[2,96,1152]{2,1,0:T(8,128)(2,1)S(1)}, bf16[2,96,1152]{2,1,0:T(8,128)(2,1)}, u32[]{:S(2)}) copy-start(bf16[2,96,1152]{2,1,0:T(8,128)(2,1)} %param.16) | copy-start | bytes 1327108
  12.2 166.9 %all-gather.35.cloned.1.call-start = ((), (), s32[]{:S(2)}) async-start(), calls=%async_computation.24 | async-start | bytes 1474560 | tf_op jit(solution)/shard_map/all_gather | solution.py:210
  12.7 196.3 %all-gather.37.cloned.1.call-start = ((), (), s32[]{:S(2)}) async-start(), calls=%async_computation.25 | async-start | bytes 1474560 | tf_op jit(solution)/shard_map/all_gather | solution.py:212
  13.3 262.2 %reduce-scatter.17.cloned.1.call-start = ((), (), s32[]{:S(2)}) async-start(), calls=%async_computation.13 | async-start | bytes 368640 | tf_op jit(solution)/shard_map/reduce_scatter | solution.py:248
  16.1 96.0 %copy-start.92 = (f32[256]{0:T(256)}, f32[256]{0:T(256)S(1)}, u32[]{:S(2)}) copy-start(f32[256]{0:T(256)S(1)} %broadcast_multiply_fusion.11) | copy-start | bytes 3076
  16.3 95.7 %copy-start.103 = (f32[256]{0:T(256)}, f32[256]{0:T(256)S(1)}, u32[]{:S(2)}) copy-start(f32[256]{0:T(256)S(1)} %add_rsqrt_fusion.3) | copy-start | bytes 3076
  17.0 91.9 %copy-start.83 = (f32[1,384]{1,0:T(1,128)}, f32[1,384]{1,0:T(1,128)S(1)}, u32[]{:S(2)}) copy-start(f32[1,384]{1,0:T(1,128)S(1)} %get-tuple-element.97) | copy-start | bytes 4612
  92.2 60.9 %copy-start.13 = (bf16[1,384,1152]{2,1,0:T(8,128)(2,1)}, bf16[1,384,1152]{2,1,0:T(8,128)(2,1)S(1)}, u32[]{:S(2)}) copy-start(bf16[1,384,1152]{2,1,0:T(8,128)(2,1)S(1)} %all-gather.12) | copy-start | bytes 2654212
  226.6 51.4 %reduce-scatter.15.cloned.1.call-start = ((), (), s32[]{:S(2)}) async-start(), calls=%async_computation.12 | async-start | bytes 368640 | tf_op jit(solution)/shard_map/reduce_scatter | solution.py:248
  238.1 70.2 %reduce-scatter.13.cloned.1.call-start = ((), (), s32[]{:S(2)}) async-start(), calls=%async_computation.11 | async-start | bytes 1105920 | tf_op jit(solution)/shard_map/reduce_scatter | solution.py:242
  240.9 97.0 %reduce-scatter.11.cloned.1.call-start = ((), (), s32[]{:S(2)}) async-start(), calls=%async_computation.10 | async-start | bytes 1105920 | tf_op jit(solution)/shard_map/reduce_scatter | solution.py:242
  246.8 122.5 %reduce-scatter.25.cloned.1.call-start = ((), (), s32[]{:S(2)}) async-start(), calls=%async_computation.17 | async-start | bytes 1474560 | tf_op jit(solution)/shard_map/reduce_scatter | solution.py:260
  250.2 151.0 %reduce-scatter.21.cloned.1.call-start = ((), (), s32[]{:S(2)}) async-start(), calls=%async_computation.15 | async-start | bytes 1474560 | tf_op jit(solution)/shard_map/reduce_scatter | solution.py:254
  253.0 179.7 %reduce-scatter.23.cloned.1.call-start = ((), (), s32[]{:S(2)}) async-start(), calls=%async_computation.16 | async-start | bytes 1474560 | tf_op jit(solution)/shard_map/reduce_scatter | solution.py:260
  256.4 208.2 %reduce-scatter.19.cloned.1.call-start = ((), (), s32[]{:S(2)}) async-start(), calls=%async_computation.14 | async-start | bytes 1474560 | tf_op jit(solution)/shard_map/reduce_scatter | solution.py:254
  259.3 241.3 %reduce-scatter.27.cloned.1.call-start = ((), (), s32[]{:S(2)}) async-start(), calls=%async_computation.18 | async-start | bytes 2211840 | tf_op jit(solution)/shard_map/reduce_scatter | solution.py:266
  267.3 268.7 %reduce-scatter.29.cloned.1.call-start = ((), (), s32[]{:S(2)}) async-start(), calls=%async_computation.19 | async-start | bytes 2211840 | tf_op jit(solution)/shard_map/reduce_scatter | solution.py:266
  267.9 344.1 %all-reduce.24.cloned.1.call-start = ((), (), s32[]{:S(2)}) async-start(), calls=%async_computation.26 | async-start | bytes 5308416 | tf_op jit(solution)/shard_map/psum | solution.py:274
  275.4 260.6 %copy-start.118 = (bf16[768]{0:T(1024)(128)(2,1)S(1)}, bf16[768]{0:T(1024)(128)(2,1)}, u32[]{:S(2)}) copy-start(bf16[768]{0:T(1024)(128)(2,1)} %pad_maximum_fusion.7) | copy-start | bytes 4612
  275.4 260.6 %copy-start.123 = (bf16[384]{0:T(512)(128)(2,1)S(1)}, bf16[384]{0:T(512)(128)(2,1)}, u32[]{:S(2)}) copy-start(bf16[384]{0:T(512)(128)(2,1)} %get-tuple-element.93) | copy-start | bytes 2308
  275.4 260.6 %copy-start.124 = (bf16[384]{0:T(512)(128)(2,1)S(1)}, bf16[384]{0:T(512)(128)(2,1)}, u32[]{:S(2)}) copy-start(bf16[384]{0:T(512)(128)(2,1)} %get-tuple-element.122) | copy-start | bytes 2308
  275.5 260.6 %copy-start.125 = (bf16[384]{0:T(512)(128)(2,1)S(1)}, bf16[384]{0:T(512)(128)(2,1)}, u32[]{:S(2)}) copy-start(bf16[384]{0:T(512)(128)(2,1)} %get-tuple-element.87) | copy-start | bytes 2308
  275.5 260.6 %copy-start.126 = (bf16[384]{0:T(512)(128)(2,1)S(1)}, bf16[384]{0:T(512)(128)(2,1)}, u32[]{:S(2)}) copy-start(bf16[384]{0:T(512)(128)(2,1)} %get-tuple-element.90) | copy-start | bytes 2308
  275.5 260.6 %copy-start.129 = (bf16[1536]{0:T(1024)(128)(2,1)S(1)}, bf16[1536]{0:T(1024)(128)(2,1)}, u32[]{:S(2)}) copy-start(bf16[1536]{0:T(1024)(128)(2,1)} %get-tuple-element.154) | copy-start | bytes 9220
  275.5 260.6 %copy-start.130 = (bf16[1536]{0:T(1024)(128)(2,1)S(1)}, bf16[1536]{0:T(1024)(128)(2,1)}, u32[]{:S(2)}) copy-start(bf16[1536]{0:T(1024)(128)(2,1)} %get-tuple-element.156) | copy-start | bytes 9220
  275.5 276.5 %copy-start.119 = (f32[384]{0:T(512)S(1)}, f32[384]{0:T(512)}, u32[]{:S(2)}) copy-start(f32[384]{0:T(512)} %fusion.53) | copy-start | bytes 4612
  275.5 306.7 %copy-start.82 = (bf16[1,384]{1,0:T(2,128)(2,1)S(1)}, bf16[1,384]{1,0:T(2,128)(2,1)}, u32[]{:S(2)}) copy-start(bf16[1,384]{1,0:T(2,128)(2,1)} %param.14) | copy-start | bytes 2308
  275.5 306.7 %copy-start.84 = (f32[1,384]{1,0:T(1,128)S(1)}, f32[1,384]{1,0:T(1,128)}, u32[]{:S(2)}) copy-start(f32[1,384]{1,0:T(1,128)} %copy-done.83) | copy-start | bytes 4612
  (130 other events, 512.2 us)
Sparse Core Ops, SparseCore 0:
  10.4 36.0 all-gather.26
  49.0 39.2 all-gather.32
  90.7 29.4 all-gather.28
  121.8 27.7 all-gather.30
  151.3 27.7 all-gather.34
  181.3 27.7 all-gather.36
  226.7 24.2 reduce-scatter.16
  253.7 24.2 reduce-scatter.14
  281.5 26.7 reduce-scatter.12
  311.1 26.6 reduce-scatter.10
  340.8 28.5 reduce-scatter.24
  372.7 28.5 reduce-scatter.20
  404.1 28.5 reduce-scatter.22
  436.1 28.5 reduce-scatter.18
  468.1 32.4 reduce-scatter.26
  503.5 32.4 reduce-scatter.28
  539.1 72.8 all-reduce.23
where the time goes:
time: 627 us; the launch traced here: 626 us
  waiting for transfers between devices  367 us (59%)
  blocking collectives  126 us (20%)
  matrix products  59.6 us (10%)
  other arithmetic  31.8 us (5%)
  local copies, waits for them, and re-layouts  20.1 us (3%)
  between operations  20 us (3%)
    reduce_scatter x2, waiting for transfers between devices, shards(): lax.psum_scatter(grads[8].astype(jnp.bfloat16), 'shard', scatter_dimensio...  71.4 us
    reduce_scatter x2, waiting for transfers between devices, shards(): lax.psum_scatter(grads[4].astype(jnp.bfloat16), 'shard', scatter_dimensio...  63.8 us
    reduce_scatter x2, waiting for transfers between devices, shards(): lax.psum_scatter(grads[6].astype(jnp.bfloat16), 'shard', scatter_dimensio...  63 us
    reduce_scatter x2, waiting for transfers between devices, shards(): lax.psum_scatter(grads[0].astype(jnp.bfloat16), 'shard', scatter_dimensio...  59.8 us
    all_gather x2, waiting for transfers between devices, shards(): lax.all_gather(w_fc2[layer_number], 'shard', axis=0, tiled=True)  53.2 us
    unnamed x2, blocking collectives  31.1 us
    psum x1, waiting for transfers between devices, shards(): lax.psum(owner_rows[0].astype(jnp.bfloat16), 'rep').astype(jnp.float32)  29.2 us
    all_gather x2, blocking collectives, shards(): lax.all_gather(w_qkv[layer_number], 'shard', axis=0, tiled=True)  28.9 us
  transfers between devices with their start and end apart: 17, of which 14 were waited for; matrix products, arithmetic and copies ran while one was open for 13% of the time, Pallas kernels for 0%

commit v1 on v0

--- a/solution.py
+++ b/solution.py
@@ -272,7 +272,9 @@
         )
         owner_rows = (
             lax.psum(owner_rows[0].astype(jnp.bfloat16), "rep").astype(jnp.float32),
-            lax.psum(owner_rows[1].astype(jnp.bfloat16), "rep").astype(jnp.float32),
+            jnp.sum(lax.all_gather(owner_rows[1].astype(jnp.bfloat16), "rep"), axis=0).astype(
+                jnp.float32
+            ),
             lax.psum(owner_rows[2].astype(jnp.bfloat16), "rep").astype(jnp.float32),
             lax.psum(owner_rows[3].astype(jnp.bfloat16), "rep").astype(jnp.float32),
             lax.psum(owner_rows[4].astype(jnp.bfloat16), "rep").astype(jnp.float32),

time: 627 us -> 627 us (level)
  waiting for transfers between devices: 367 us -> 345 us
  local copies, waits for them, and re-layouts: 20.1 us -> 38.8 us
    unnamed x2 -> x3, blocking collectives: 31.1 us -> 62.6 us
    psum x1 -> x0, blocking collectives: 27 us -> none  [shards(): lax.psum(owner_rows[1].astype(jnp.bfloat16), 'rep').astype(jnp.float32)]
    reduce_scatter x2, waiting for transfers between devices: 59.8 us -> 47.7 us  [shards(): lax.psum_scatter(grads[0].astype(jnp.bfloat16), 'shard', scatter_dimensio...]
    psum x1, waiting for transfers between devices: 29.2 us -> 20.9 us  [shards(): lax.psum(owner_rows[0].astype(jnp.bfloat16), 'rep').astype(jnp.float32)]
    unnamed x325 -> x352, local copies, waits for them, and re-layouts: 9.73 us -> 17.9 us
  transfers between devices with their start and end apart: 17 -> 17, of which waited for: 14 -> 13; matrix products, arithmetic and copies ran while one was open for 13% -> 16% of each run, Pallas kernels for 0% -> 0%
where the time goes in v1:
time: 627 us; the launch traced here: 626 us
  waiting for transfers between devices  345 us (55%)
  blocking collectives  130 us (21%)
  matrix products  59.8 us (10%)
  local copies, waits for them, and re-layouts  38.8 us (6%)
  other arithmetic  30 us (5%)
  between operations  21.2 us (3%)
    reduce_scatter x2, waiting for transfers between devices, shards(): lax.psum_scatter(grads[8].astype(jnp.bfloat16), 'shard', scatter_dimensio...  71.3 us
    reduce_scatter x2, waiting for transfers between devices, shards(): lax.psum_scatter(grads[4].astype(jnp.bfloat16), 'shard', scatter_dimensio...  63.8 us
    reduce_scatter x2, waiting for transfers between devices, shards(): lax.psum_scatter(grads[6].astype(jnp.bfloat16), 'shard', scatter_dimensio...  63 us
    unnamed x3, blocking collectives  62.6 us
    all_gather x2, waiting for transfers between devices, shards(): lax.all_gather(w_fc2[layer_number], 'shard', axis=0, tiled=True)  53.2 us
    reduce_scatter x2, waiting for transfers between devices, shards(): lax.psum_scatter(grads[0].astype(jnp.bfloat16), 'shard', scatter_dimensio...  47.7 us
    all_gather x2, blocking collectives, shards(): lax.all_gather(w_qkv[layer_number], 'shard', axis=0, tiled=True)  28.8 us
    all_gather x2, waiting for transfers between devices, shards(): lax.all_gather(w_fc1[layer_number], 'shard', axis=0, tiled=True)  22 us
  transfers between devices with their start and end apart: 17, of which 13 were waited for; matrix products, arithmetic and copies ran while one was open for 16% of the time, Pallas kernels for 0%

profile of v1, /device:TPU:0, one launch (start us, length us, event | category | flops | bytes accessed | tf_op | source)
XLA Modules:
  0.0 625.6 jit_solution(659307407894853339)
XLA Ops:
  17.1 9.5 %all-gather.17 = bf16[1,1536]{1,0:T(2,128)(2,1)S(1)} all-gather(bf16[1,384]{1,0:T(2,128)(2,1)S(1)} %get-tuple-element.131), channel_id=19, replica_groups=mesh['shard'=4,'rep'=8] {'shard'}, dimensions={1}, use_global_device_ids=true | all-gather | bytes 3840 | tf_op jit(solution)/shard_map/all_gather | solution.py:211
  27.3 8.0 %all-gather.7 = bf16[1,1536]{1,0:T(2,128)(2,1)S(1)} all-gather(bf16[1,384]{1,0:T(2,128)(2,1)S(1)} %get-tuple-element.132), channel_id=9, replica_groups=mesh['shard'=4,'rep'=8] {'shard'}, dimensions={1}, use_global_device_ids=true | all-gather | bytes 3840 | tf_op jit(solution)/shard_map/all_gather | solution.py:211
  37.6 15.8 %all-reduce.23 = (bf16[2304]{0:T(1024)(128)(2,1)S(1)}, bf16[768]{0:T(1024)(128)(2,1)S(1)}, bf16[384]{0:T(512)(128)(2,1)S(1)}, bf16[384]{0:T(512)(128)(2,1)S(1)},...) all-reduce(bf16[2304]{0:T(1024)(128)(2,1)S(1)} %dynamic-update-slic, ...), channel_id=3, replica_groups=mesh['shard'=4,'rep'=8] {'shard'}, use_global_device_ids=true, to_apply=%add | all-reduce | flops 7680 | bytes 30720
  56.4 10.2 %all-gather.14 = bf16[1,384,384]{2,1,0:T(8,128)(2,1)} all-gather(bf16[1,96,384]{2,1,0:T(8,128)(2,1)S(1)} %get-tuple-element.123), channel_id=16, replica_groups=mesh['shard'=4,'rep'=8] {'shard'}, dimensions={1}, use_global_device_ids=true | all-gather | bytes 368640 | tf_op jit(solution)/shard_map/all_gather | solution.py:208
  66.6 11.1 %all-gather.4 = bf16[1,384,384]{2,1,0:T(8,128)(2,1)S(1)} all-gather(bf16[1,96,384]{2,1,0:T(8,128)(2,1)S(1)} %get-tuple-element.124), channel_id=6, replica_groups=mesh['shard'=4,'rep'=8] {'shard'}, dimensions={1}, use_global_device_ids=true | all-gather | bytes 368640 | tf_op jit(solution)/shard_map/all_gather | solution.py:208
  77.8 14.5 %all-gather.12 = bf16[1,384,1152]{2,1,0:T(8,128)(2,1)S(1)} all-gather(bf16[1,96,1152]{2,1,0:T(8,128)(2,1)S(1)} %get-tuple-element.114), channel_id=14, replica_groups=mesh['shard'=4,'rep'=8] {'shard'}, dimensions={1}, use_global_device_ids=true | all-gather | bytes 1105920 | tf_op jit(solution)/shard_map/all_gather | solution.py:206
  92.3 14.3 %all-gather.2 = bf16[1,384,1152]{2,1,0:T(8,128)(2,1)S(1)} all-gather(bf16[1,96,1152]{2,1,0:T(8,128)(2,1)S(1)} %get-tuple-element.115), channel_id=4, replica_groups=mesh['shard'=4,'rep'=8] {'shard'}, dimensions={1}, use_global_device_ids=true | all-gather | bytes 1105920 | tf_op jit(solution)/shard_map/all_gather | solution.py:206
  115.6 4.5 all-gather.31.cloned.1.call-done
  120.1 3.0 convolution_add_fusion.1
  123.2 26.4 %all-gather.33.cloned.1.call-done = bf16[1,1536,384]{2,1,0:T(8,128)(2,1)} async-done(((bf16[1,384,384]{2,1,0:T(8,128)(2,1)}), bf16[1,1536,384]{2,1,0:T(8,128)(2,1)}) %all-gather.33.cloned.1.call-update) | async-done | bytes 1179664 | tf_op jit(solution)/shard_map/all_gather | solution.py:212
  149.6 3.2 fusion.152
  161.5 17.5 %all-gather.37.cloned.1.call-done = bf16[1,384,1536]{2,1,0:T(8,128)(2,1)} async-done(((bf16[1,96,1536]{2,1,0:T(8,128)(2,1)}), bf16[1,384,1536]{2,1,0:T(8,128)(2,1)}) %all-gather.37.cloned.1.call-update) | async-done | bytes 1179664 | tf_op jit(solution)/shard_map/all_gather | solution.py:210
  179.0 3.2 convolution_add_fusion
  182.2 26.9 %all-gather.39.cloned.1.call-done = bf16[1,1536,384]{2,1,0:T(8,128)(2,1)} async-done(((bf16[1,384,384]{2,1,0:T(8,128)(2,1)}), bf16[1,1536,384]{2,1,0:T(8,128)(2,1)}) %all-gather.39.cloned.1.call-update) | async-done | bytes 1179664 | tf_op jit(solution)/shard_map/all_gather | solution.py:212
  209.0 4.0 fusion.165
  226.8 2.5 fusion.87
  238.1 2.6 convolution_convert_fusion
  246.8 3.3 convolution_convert_fusion.2
  253.0 3.2 convolution_convert_fusion.3
  256.4 2.8 convolution_convert_fusion.5
  264.3 2.8 multiply_convert_fusion.1
  272.5 16.1 %all-reduce.22 = (bf16[768]{0:T(1024)(128)(2,1)}, bf16[768]{0:T(1024)(128)(2,1)}, bf16[384]{0:T(512)(128)(2,1)S(1)}, bf16[384]{0:T(512)(128)(2,1)S(1)}, bf16[153...) all-reduce(bf16[768]{0:T(1024)(128)(2,1)S(1)} %pad_maximum_fusion.7, ...), channel_id=27, replica_groups=mesh['shard'=4,'rep'=8] {'shard'}, use_global_device_ids=true, to_apply=%region_42.43.clone | all-reduce | flops 10752 | bytes 43008
  290.0 18.2 %reduce-scatter.13.cloned.1.call-done = bf16[96,1152]{1,0:T(8,128)(2,1)} async-done(((bf16[384,1152]{1,0:T(8,128)(2,1)}), bf16[96,1152]{1,0:T(8,128)(2,1)}) %reduce-scatter.13.cloned.1.call-update) | async-done | bytes 221200 | tf_op jit(solution)/shard_map/reduce_scatter | solution.py:242
  308.2 29.5 %reduce-scatter.11.cloned.1.call-done = bf16[96,1152]{1,0:T(8,128)(2,1)} async-done(((bf16[384,1152]{1,0:T(8,128)(2,1)}), bf16[96,1152]{1,0:T(8,128)(2,1)}) %reduce-scatter.11.cloned.1.call-update) | async-done | bytes 221200 | tf_op jit(solution)/shard_map/reduce_scatter | solution.py:242
  337.7 31.5 %reduce-scatter.25.cloned.1.call-done = bf16[384,384]{1,0:T(8,128)(2,1)} async-done(((bf16[1536,384]{1,0:T(8,128)(2,1)}), bf16[384,384]{1,0:T(8,128)(2,1)}) %reduce-scatter.25.cloned.1.call-update) | async-done | bytes 294928 | tf_op jit(solution)/shard_map/reduce_scatter | solution.py:260
  369.2 31.9 %reduce-scatter.21.cloned.1.call-done = bf16[96,1536]{1,0:T(8,128)(2,1)} async-done(((bf16[384,1536]{1,0:T(8,128)(2,1)}), bf16[96,1536]{1,0:T(8,128)(2,1)}) %reduce-scatter.21.cloned.1.call-update) | async-done | bytes 294928 | tf_op jit(solution)/shard_map/reduce_scatter | solution.py:254
  401.1 31.5 %reduce-scatter.23.cloned.1.call-done = bf16[384,384]{1,0:T(8,128)(2,1)} async-done(((bf16[1536,384]{1,0:T(8,128)(2,1)}), bf16[384,384]{1,0:T(8,128)(2,1)}) %reduce-scatter.23.cloned.1.call-update) | async-done | bytes 294928 | tf_op jit(solution)/shard_map/reduce_scatter | solution.py:260
  432.6 31.9 %reduce-scatter.19.cloned.1.call-done = bf16[96,1536]{1,0:T(8,128)(2,1)} async-done(((bf16[384,1536]{1,0:T(8,128)(2,1)}), bf16[96,1536]{1,0:T(8,128)(2,1)}) %reduce-scatter.19.cloned.1.call-update) | async-done | bytes 294928 | tf_op jit(solution)/shard_map/reduce_scatter | solution.py:254
  464.5 36.0 %reduce-scatter.27.cloned.1.call-done = bf16[96,2304]{1,0:T(8,128)(2,1)} async-done(((bf16[384,2304]{1,0:T(8,128)(2,1)}), bf16[96,2304]{1,0:T(8,128)(2,1)}) %reduce-scatter.27.cloned.1.call-update) | async-done | bytes 442384 | tf_op jit(solution)/shard_map/reduce_scatter | solution.py:266
  500.4 35.4 %reduce-scatter.29.cloned.1.call-done = bf16[96,2304]{1,0:T(8,128)(2,1)} async-done(((bf16[384,2304]{1,0:T(8,128)(2,1)}), bf16[96,2304]{1,0:T(8,128)(2,1)}) %reduce-scatter.29.cloned.1.call-update) | async-done | bytes 442384 | tf_op jit(solution)/shard_map/reduce_scatter | solution.py:266
  550.0 30.7 %all-reduce.20 = (bf16[1536]{0:T(1024)(128)(2,1)}, bf16[1536]{0:T(1024)(128)(2,1)}, bf16[1,96]{1,0:T(2,128)(2,1)}, bf16[1,96]{1,0:T(2,128)(2,1)}, bf16[1,384]{1,...) all-reduce(bf16[1536]{0:T(1024)(128)(2,1)S(1)} %dynamic-update-slic, ...), channel_id=23, replica_groups=mesh['shard'=4,'rep'=8] {'rep'}, use_global_device_ids=true, to_apply=%add.9 | all-reduce | flops 5376 | bytes 21504
  590.8 20.9 %all-reduce.26.cloned.1.call-done = (bf16[1,96,1152]{2,1,0:T(8,128)(2,1)}, bf16[1,96,1152]{2,1,0:T(8,128)(2,1)}, bf16[1,96,384]{2,1,0:T(8,128)(2,1)}, bf16[1,96,...) async-done(((bf16[1,96,1152]{2,1,0:T(8,128)(2,1)}, ...) | async-done | bytes 2654224 | tf_op jit(solution)/shard_map/psum | solution.py:274
  (534 shorter events, 101.4 us)
Async XLA Ops:
  7.2 99.4 %all-gather.29.cloned.1.call-start = ((), (), s32[]{:S(2)}) async-start(), calls=%async_computation.20 | async-start | bytes 2211840 | tf_op jit(solution)/shard_map/all_gather | solution.py:214
  9.4 99.4 %all-gather.35.cloned.1.call-start = ((), (), s32[]{:S(2)}) async-start(), calls=%async_computation.23 | async-start | bytes 2211840 | tf_op jit(solution)/shard_map/all_gather | solution.py:214
  10.2 109.9 %all-gather.31.cloned.1.call-start = ((), (), s32[]{:S(2)}) async-start(), calls=%async_computation.21 | async-start | bytes 1474560 | tf_op jit(solution)/shard_map/all_gather | solution.py:210
  11.1 45.2 %copy-start.67 = (bf16[2,96,384]{2,1,0:T(8,128)(2,1)S(1)}, bf16[2,96,384]{2,1,0:T(8,128)(2,1)}, u32[]{:S(2)}) copy-start(bf16[2,96,384]{2,1,0:T(8,128)(2,1)} %param.18) | copy-start | bytes 442372
  11.2 138.4 %all-gather.33.cloned.1.call-start = ((), (), s32[]{:S(2)}) async-start(), calls=%async_computation.22 | async-start | bytes 1474560 | tf_op jit(solution)/shard_map/all_gather | solution.py:212
  12.1 65.6 %copy-start.55 = (bf16[2,96,1152]{2,1,0:T(8,128)(2,1)S(1)}, bf16[2,96,1152]{2,1,0:T(8,128)(2,1)}, u32[]{:S(2)}) copy-start(bf16[2,96,1152]{2,1,0:T(8,128)(2,1)} %param.16) | copy-start | bytes 1327108
  12.2 166.8 %all-gather.37.cloned.1.call-start = ((), (), s32[]{:S(2)}) async-start(), calls=%async_computation.24 | async-start | bytes 1474560 | tf_op jit(solution)/shard_map/all_gather | solution.py:210
  12.8 196.3 %all-gather.39.cloned.1.call-start = ((), (), s32[]{:S(2)}) async-start(), calls=%async_computation.25 | async-start | bytes 1474560 | tf_op jit(solution)/shard_map/all_gather | solution.py:212
  13.3 276.6 %reduce-scatter.17.cloned.1.call-start = ((), (), s32[]{:S(2)}) async-start(), calls=%async_computation.13 | async-start | bytes 368640 | tf_op jit(solution)/shard_map/reduce_scatter | solution.py:248
  16.1 95.8 %copy-start.95 = (f32[256]{0:T(256)}, f32[256]{0:T(256)S(1)}, u32[]{:S(2)}) copy-start(f32[256]{0:T(256)S(1)} %broadcast_multiply_fusion.11) | copy-start | bytes 3076
  16.4 95.6 %copy-start.106 = (f32[256]{0:T(256)}, f32[256]{0:T(256)S(1)}, u32[]{:S(2)}) copy-start(f32[256]{0:T(256)S(1)} %add_rsqrt_fusion.3) | copy-start | bytes 3076
  17.1 91.7 %copy-start.86 = (f32[1,384]{1,0:T(1,128)}, f32[1,384]{1,0:T(1,128)S(1)}, u32[]{:S(2)}) copy-start(f32[1,384]{1,0:T(1,128)S(1)} %get-tuple-element.97) | copy-start | bytes 4612
  77.7 36.6 %copy-start.14 = (bf16[1,384,384]{2,1,0:T(8,128)(2,1)}, bf16[1,384,384]{2,1,0:T(8,128)(2,1)S(1)}, u32[]{:S(2)}) copy-start(bf16[1,384,384]{2,1,0:T(8,128)(2,1)S(1)} %all-gather.4) | copy-start | bytes 884740
  92.3 60.7 %copy-start.13 = (bf16[1,384,1152]{2,1,0:T(8,128)(2,1)}, bf16[1,384,1152]{2,1,0:T(8,128)(2,1)S(1)}, u32[]{:S(2)}) copy-start(bf16[1,384,1152]{2,1,0:T(8,128)(2,1)S(1)} %all-gather.12) | copy-start | bytes 2654212
  111.3 41.7 %copy-start.75 = (f32[384]{0:T(512)}, f32[384]{0:T(512)S(1)}, u32[]{:S(2)}) copy-start(f32[384]{0:T(512)S(1)} %get-tuple-element.33) | copy-start | bytes 4612
  111.9 8.2 %copy-start.68 = (f32[384]{0:T(512)}, f32[384]{0:T(512)S(1)}, u32[]{:S(2)}) copy-start(f32[384]{0:T(512)S(1)} %get-tuple-element.37) | copy-start | bytes 4612
  115.4 7.8 %copy-start.79 = (f32[256]{0:T(256)}, f32[256]{0:T(256)S(1)}, u32[]{:S(2)}) copy-start(f32[256]{0:T(256)S(1)} %broadcast_multiply_fusion.10) | copy-start | bytes 3076
  120.1 29.4 %copy-start.119 = (f32[384]{0:T(512)S(1)}, f32[384]{0:T(512)}, u32[]{:S(2)}) copy-start(f32[384]{0:T(512)} %get-tuple-element.35) | copy-start | bytes 4612
  120.1 29.4 %copy-start.138 = (f32[384]{0:T(512)S(1)}, f32[384]{0:T(512)}, u32[]{:S(2)}) copy-start(f32[384]{0:T(512)} %convert_element_type.433) | copy-start | bytes 4612
  226.6 63.4 %reduce-scatter.15.cloned.1.call-start = ((), (), s32[]{:S(2)}) async-start(), calls=%async_computation.12 | async-start | bytes 368640 | tf_op jit(solution)/shard_map/reduce_scatter | solution.py:248
  238.1 70.1 %reduce-scatter.13.cloned.1.call-start = ((), (), s32[]{:S(2)}) async-start(), calls=%async_computation.11 | async-start | bytes 1105920 | tf_op jit(solution)/shard_map/reduce_scatter | solution.py:242
  240.8 96.9 %reduce-scatter.11.cloned.1.call-start = ((), (), s32[]{:S(2)}) async-start(), calls=%async_computation.10 | async-start | bytes 1105920 | tf_op jit(solution)/shard_map/reduce_scatter | solution.py:242
  246.7 122.4 %reduce-scatter.25.cloned.1.call-start = ((), (), s32[]{:S(2)}) async-start(), calls=%async_computation.17 | async-start | bytes 1474560 | tf_op jit(solution)/shard_map/reduce_scatter | solution.py:260
  250.2 150.9 %reduce-scatter.21.cloned.1.call-start = ((), (), s32[]{:S(2)}) async-start(), calls=%async_computation.15 | async-start | bytes 1474560 | tf_op jit(solution)/shard_map/reduce_scatter | solution.py:254
  252.9 179.6 %reduce-scatter.23.cloned.1.call-start = ((), (), s32[]{:S(2)}) async-start(), calls=%async_computation.16 | async-start | bytes 1474560 | tf_op jit(solution)/shard_map/reduce_scatter | solution.py:260
  256.3 208.2 %reduce-scatter.19.cloned.1.call-start = ((), (), s32[]{:S(2)}) async-start(), calls=%async_computation.14 | async-start | bytes 1474560 | tf_op jit(solution)/shard_map/reduce_scatter | solution.py:254
  259.3 241.2 %reduce-scatter.27.cloned.1.call-start = ((), (), s32[]{:S(2)}) async-start(), calls=%async_computation.18 | async-start | bytes 2211840 | tf_op jit(solution)/shard_map/reduce_scatter | solution.py:266
  267.2 268.6 %reduce-scatter.29.cloned.1.call-start = ((), (), s32[]{:S(2)}) async-start(), calls=%async_computation.19 | async-start | bytes 2211840 | tf_op jit(solution)/shard_map/reduce_scatter | solution.py:266
  267.8 343.9 %all-reduce.26.cloned.1.call-start = ((), (), s32[]{:S(2)}) async-start(), calls=%async_computation.26 | async-start | bytes 5308416 | tf_op jit(solution)/shard_map/psum | solution.py:274
  272.4 312.7 %copy-start.4 = (bf16[1,384,2304]{2,1,0:T(8,128)(2,1)S(1)}, bf16[1,384,2304]{2,1,0:T(8,128)(2,1)}, u32[]{:S(2)}) copy-start(bf16[1,384,2304]{2,1,0:T(8,128)(2,1)} %all-gather.35.cloned.1.call-done) | copy-start | bytes 5308420
  535.8 50.7 %copy-start.3 = (bf16[1,384,2304]{2,1,0:T(8,128)(2,1)S(1)}, bf16[1,384,2304]{2,1,0:T(8,128)(2,1)}, u32[]{:S(2)}) copy-start(bf16[1,384,2304]{2,1,0:T(8,128)(2,1)} %all-gather.29.cloned.1.call-done) | copy-start | bytes 5308420
  538.5 48.1 %copy-start.70 = (bf16[2304,1]{0,1:T(2,128)(2,1)S(1)}, bf16[2304,1]{0,1:T(2,128)(2,1)}, u32[]{:S(2)}) copy-start(bf16[2304,1]{0,1:T(2,128)(2,1)} %reshape.1088) | copy-start | bytes 13828
  (141 other events, 369.7 us)
Sparse Core Ops, SparseCore 0:
  10.4 36.0 all-gather.28
  49.0 39.2 all-gather.34
  90.7 29.3 all-gather.30
  121.8 27.7 all-gather.32
  151.2 27.7 all-gather.36
  181.3 27.7 all-gather.38
  226.7 24.1 reduce-scatter.16
  253.7 24.2 reduce-scatter.14
  281.5 26.6 reduce-scatter.12
  311.0 26.6 reduce-scatter.10
  340.6 28.5 reduce-scatter.24
  372.5 28.5 reduce-scatter.20
  404.0 28.5 reduce-scatter.22
  435.9 28.5 reduce-scatter.18
  467.9 32.4 reduce-scatter.26
  503.3 32.4 reduce-scatter.28
  538.9 72.7 all-reduce.25
